TPU v7x, 32 devices: a whole 2x2x4 slice. The times are simulated.
32 devices in a mesh: section: 8 (over z, core), tensor: 2 (over x), replica: 2 (over y).
Axes of the slice: x: 2, y: 2, z: 4, core: 2. Of those that a mesh axis runs over, the one named last changes fastest.
Arguments:
- pool_inputs: bfloat16 [8, 256, 2, 1408], P('section', 'replica', None, 'tensor'), may hold values from -6 to 6
- pool_mixed: bfloat16 [8, 256, 1408], P('section', 'replica'), may hold values from -6 to 6
- crop_ids: int32 [8, 8, 128], P('section', 'replica'), may hold values from 0 to 127
- incoming: bfloat16 [8, 256, 1408], P('section', 'replica', 'tensor'), may hold values from -6 to 6
- loss_grads: bfloat16 [3, 256, 1408], P(None, 'replica', 'tensor'), may hold values from -6 to 6
- w_proj: bfloat16 [8, 2, 1408, 1408], P('section', None, ('tensor', 'replica')), may hold values from -0.109375 to 0.109375
- w_up: bfloat16 [8, 1408, 3072], P('section', None, ('tensor', 'replica')), may hold values from -0.15625 to 0.15625
- w_down: bfloat16 [8, 3072, 1408], P('section', ('tensor', 'replica')), may hold values from -0.109375 to 0.109375
Outputs:
- grad_proj: bfloat16 [8, 2, 1408, 1408], P('section', None, ('tensor', 'replica'))
- grad_up: bfloat16 [8, 1408, 3072], P('section', None, ('tensor', 'replica'))
- grad_down: bfloat16 [8, 3072, 1408], P('section', ('tensor', 'replica'))
- outgoing: bfloat16 [8, 256, 2, 1408], P('section', 'replica', None, 'tensor')
All inputs are finite; a program needn't handle non-finite values.
Results may differ from a plain program's by a relative error of at most 0.02.
Values may be sent and summed in bfloat16 or wider, within the bound.
A program may use at most 128 MiB of HBM per device.

v0:
```python
import jax
import jax.numpy as jnp
from jax import lax
from jax.sharding import PartitionSpec as P

gelu_scale = 0.7978845608
gelu_cubic = 0.044715


def from_partner(value, axis, bit):
    mask = 2**bit
    pairs = [(source, source ^ mask) for source in range(lax.axis_size(axis))]
    return lax.ppermute(value, axis, pairs)


def shifted(x, axis, by):
    devices = lax.axis_size(axis)
    pairs = [(i, i + by) for i in range(devices) if 0 <= i + by < devices]
    return lax.ppermute(x, axis, pairs)


def gelu_pair(pre_gelu):
    inner = gelu_scale * (pre_gelu + gelu_cubic * pre_gelu * pre_gelu * pre_gelu)
    tanh_part = jnp.tanh(inner)
    gelu_value = 0.5 * pre_gelu * (1.0 + tanh_part)
    gelu_slope = 0.5 * (1.0 + tanh_part) + 0.5 * pre_gelu * (
        1.0 - tanh_part * tanh_part
    ) * gelu_scale * (1.0 + 3.0 * gelu_cubic * pre_gelu * pre_gelu)
    return (gelu_value, gelu_slope)


def reflect(block, section_count):
    for bit_number in range(section_count.bit_length() - 1):
        block = from_partner(block, "section", bit_number)
    return block


def body(pool_inputs, pool_mixed, crop_ids, incoming, loss_grads, w_proj, w_up, w_down):
    section_index = lax.axis_index("section")
    section_count = lax.axis_size("section")
    proj_full, up_full, down_full = (
        lax.all_gather(w_proj, "replica", axis=2, tiled=True),
        lax.all_gather(w_up, "replica", axis=2, tiled=True),
        lax.all_gather(w_down, "replica", axis=1, tiled=True),
    )
    proj_local = proj_full[0]
    up_local = up_full[0]
    down_local = down_full[0]
    seed_full, loss_full = (
        lax.all_gather(incoming, "tensor", axis=2, tiled=True),
        lax.all_gather(loss_grads, "tensor", axis=2, tiled=True),
    )
    encoder = section_index < section_count // 2
    decoder_flag = jnp.where(encoder, 0.0, 1.0).astype(jnp.bfloat16)
    skip_mask = jnp.stack([jnp.ones((), jnp.bfloat16), decoder_flag])[None, :, None]
    encoder_weight = jnp.where(encoder, 1.0, 0.0).astype(jnp.float32)
    is_top = section_index == section_count - 1
    tick_count = crop_ids.shape[1]
    upstream = seed_full[0]
    kept_inputs, kept_mixed, kept_active, kept_hidden, kept_grads, kept_upstream = (
        [],
        [],
        [],
        [],
        [],
        [],
    )
    input_grad = None
    for tick_index in range(tick_count):
        picked_rows = crop_ids[0, tick_index]
        inputs = pool_inputs[0][picked_rows] * skip_mask
        mixed_rows = pool_mixed[0][picked_rows]
        pre_gelu = jnp.dot(mixed_rows, up_local, preferred_element_type=jnp.float32)
        gelu_value, gelu_slope = gelu_pair(pre_gelu)
        activated = gelu_value.astype(jnp.bfloat16)
        back_act = jnp.einsum("md,fd->mf", upstream, down_local, preferred_element_type=jnp.float32)
        back_hidden = (back_act * gelu_slope).astype(jnp.bfloat16)
        partial_back = jnp.einsum(
            "mf,df->md", back_hidden, up_local, preferred_element_type=jnp.float32
        )
        back_mixed = upstream.astype(jnp.float32) + lax.psum(partial_back, "tensor")
        mixed_grad = back_mixed.astype(jnp.bfloat16)
        input_grad = jnp.einsum(
            "mj,kij->mki", mixed_grad, proj_local, preferred_element_type=jnp.float32
        ).astype(jnp.bfloat16)
        kept_inputs.append(inputs)
        kept_mixed.append(mixed_rows)
        kept_active.append(activated)
        kept_hidden.append(back_hidden)
        kept_grads.append(mixed_grad)
        kept_upstream.append(upstream)
        if tick_index + 1 < tick_count:
            from_above = shifted(input_grad[:, 0], "section", -1)
            mirrored = reflect(input_grad[:, 1], section_count)
            summed = (
                from_above.astype(jnp.float32) + encoder_weight * mirrored.astype(jnp.float32)
            ).astype(jnp.bfloat16)
            summed = lax.all_gather(summed, "tensor", axis=1, tiled=True)
            upstream = jnp.where(is_top, loss_full[tick_index], summed)
    all_inputs = jnp.concatenate(kept_inputs, axis=0)
    all_mixed = jnp.concatenate(kept_mixed, axis=0)
    all_active = jnp.concatenate(kept_active, axis=0)
    all_hidden = jnp.concatenate(kept_hidden, axis=0)
    all_grads = jnp.concatenate(kept_grads, axis=0)
    all_upstream = jnp.concatenate(kept_upstream, axis=0)
    down_total = jnp.einsum(
        "mf,md->fd", all_active, all_upstream, preferred_element_type=jnp.float32
    )
    up_total = jnp.einsum("md,mf->df", all_mixed, all_hidden, preferred_element_type=jnp.float32)
    proj_total = jnp.einsum(
        "mki,mj->kij", all_inputs, all_grads, preferred_element_type=jnp.float32
    )
    reduced = (
        lax.psum_scatter(
            proj_total[None].astype(jnp.bfloat16), "replica", scatter_dimension=2, tiled=True
        ).astype(jnp.float32),
        lax.psum_scatter(
            up_total[None].astype(jnp.bfloat16), "replica", scatter_dimension=2, tiled=True
        ).astype(jnp.float32),
        lax.psum_scatter(
            down_total[None].astype(jnp.bfloat16), "replica", scatter_dimension=1, tiled=True
        ).astype(jnp.float32),
    )
    return (
        reduced[0].astype(jnp.bfloat16),
        reduced[1].astype(jnp.bfloat16),
        reduced[2].astype(jnp.bfloat16),
        input_grad[None],
    )


def solution(mesh):
    in_specs = (
        P("section", "replica", None, "tensor"),
        P("section", "replica", None),
        P("section", "replica", None),
        P("section", "replica", "tensor"),
        P(None, "replica", "tensor"),
        P("section", None, ("tensor", "replica"), None),
        P("section", None, ("tensor", "replica")),
        P("section", ("tensor", "replica"), None),
    )
    out_specs = (
        P("section", None, ("tensor", "replica"), None),
        P("section", None, ("tensor", "replica")),
        P("section", ("tensor", "replica"), None),
        P("section", "replica", None, "tensor"),
    )
    return jax.shard_map(body, mesh=mesh, in_specs=in_specs, out_specs=out_specs, check_vma=False)
```

profile of v0, /device:TPU:0, one launch (start us, length us, event | category | flops | bytes accessed | tf_op | source)
XLA Modules:
  0.0 637.9 jit_solution(14734872152342492354)
XLA Ops:
  9.7 8.2 %all_gather.24 = bf16[1,128,1408]{1,2,0:T(8,128)(2,1)S(1)} all-gather(bf16[1,128,704]{1,2,0:T(8,128)(2,1)S(1)} %copy-done.23), channel_id=1, replica_groups=mesh['section'=8,'tensor'=2,'replica'=2] {'tensor'}, dimensions={2}, use_global_device_ids=true | all-gather | bytes 540672 | tf_op jit(solution)/shard_map/all_gather | solution.py:50
  17.9 52.6 %all-gather.7.cloned.1.call-done = bf16[1,1408,1536]{2,1,0:T(8,128)(2,1)} async-done(((bf16[1,1408,768]{2,1,0:T(8,128)(2,1)}), bf16[1,1408,1536]{2,1,0:T(8,128)(2,1)}) %all-gather.7.cloned.1.call-update) | async-done | bytes 4325392 | tf_op jit(solution)/shard_map/all_gather | solution.py:43
  70.5 4.0 multiply_convert_fusion.3
  74.5 55.8 %all-gather.5.cloned.1.call-done = bf16[1,1536,1408]{2,1,0:T(8,128)(2,1)} async-done(((bf16[1,768,1408]{2,1,0:T(8,128)(2,1)}), bf16[1,1536,1408]{2,1,0:T(8,128)(2,1)}) %all-gather.5.cloned.1.call-update) | async-done | bytes 4325392 | tf_op jit(solution)/shard_map/all_gather | solution.py:44
  130.3 4.0 fusion.56
  138.9 31.7 %all-reduce.5.cloned.1.call-done = f32[128,1408]{1,0:T(8,128)} async-done(((f32[128,1408]{1,0:T(8,128)}), f32[128,1408]{1,0:T(8,128)}) %all-reduce.5.cloned.1.call-update) | async-done | bytes 720912 | tf_op jit(solution)/shard_map/psum | solution.py:81
  171.7 54.4 %all-gather.11.cloned.1.call-done = bf16[1,2,704,1408]{3,2,1,0:T(8,128)(2,1)} async-done(((bf16[1,2,352,1408]{3,2,1,0:T(8,128)(2,1)}), bf16[1,2,704,1408]{3,2,1,0:T(8,128)(2,1)}) %all-gather.11.cloned.1.call-update) | async-done | bytes 3964944 | tf_op jit(solution)/shard_map/all_gather | solution.py:42
  232.4 16.7 %all-gather.9.cloned.1.call-done = bf16[3,128,1408]{1,2,0:T(8,128)(2,1)} async-done(((bf16[3,128,704]{1,2,0:T(8,128)(2,1)}), bf16[3,128,1408]{1,2,0:T(8,128)(2,1)}) %all-gather.9.cloned.1.call-update) | async-done | bytes 1081360 | tf_op jit(solution)/shard_map/all_gather | solution.py:51
  255.1 4.2 multiply_convert_fusion.2
  259.2 6.9 %collective-permute-done.3 = bf16[128,704]{0,1:T(8,128)(2,1)S(1)} collective-permute-done((bf16[128,704]{0,1:T(8,128)(2,1)S(1)}, bf16[128,704]{0,1:T(8,128)(2,1)S(1)}, u32[]{:S(2)}, u32[]{:S(2)}) %collective-permute-start.3) | collective-permute-done | bytes 180256 | tf_op jit(solution)/shard_map/ppermute | solution.py:13
  266.2 6.2 all_gather.29
  272.7 4.2 fusion.53
  280.1 32.3 %all-reduce.7.cloned.1.call-done = f32[128,1408]{1,0:T(8,128)} async-done(((f32[128,1408]{1,0:T(8,128)}), f32[128,1408]{1,0:T(8,128)}) %all-reduce.7.cloned.1.call-update) | async-done | bytes 720912 | tf_op jit(solution)/shard_map/psum | solution.py:81
  313.6 3.5 fusion.103
  327.6 4.1 multiply_convert_fusion.1
  331.7 5.0 collective-permute-done.7
  336.7 6.4 %all_gather.30 = bf16[128,1408]{0,1:T(8,128)(2,1)S(1)} all-gather(bf16[128,704]{0,1:T(8,128)(2,1)S(1)} %add_convert_fusion.5), channel_id=1, replica_groups=mesh['section'=8,'tensor'=2,'replica'=2] {'tensor'}, dimensions={1}, use_global_device_ids=true | all-gather | bytes 540672 | tf_op jit(solution)/shard_map/all_gather | solution.py:98
  343.4 4.2 fusion.50
  350.9 32.9 %all-reduce.9.cloned.1.call-done = f32[128,1408]{1,0:T(8,128)} async-done(((f32[128,1408]{1,0:T(8,128)}), f32[128,1408]{1,0:T(8,128)}) %all-reduce.9.cloned.1.call-update) | async-done | bytes 720912 | tf_op jit(solution)/shard_map/psum | solution.py:81
  385.0 3.4 fusion.106
  399.0 4.1 multiply_convert_fusion
  403.1 5.0 collective-permute-done.11
  408.2 6.2 all_gather.31
  414.6 4.2 fusion.47
  432.3 22.7 %all-reduce.11.cloned.1.call-done = f32[128,1408]{1,0:T(8,128)} async-done(((f32[128,1408]{1,0:T(8,128)}), f32[128,1408]{1,0:T(8,128)}) %all-reduce.11.cloned.1.call-update) | async-done | bytes 720912 | tf_op jit(solution)/shard_map/psum | solution.py:81
  456.3 5.7 fusion.34
  463.6 5.6 fusion
  470.8 4.6 fusion.1
  475.4 4.2 fusion.112
  479.6 34.5 %reduce-scatter.4.cloned.1.call-done = bf16[1,2,352,1408]{3,2,1,0:T(8,128)(2,1)} async-done(((bf16[1,2,704,1408]{3,2,1,0:T(8,128)(2,1)}), bf16[1,2,352,1408]{3,2,1,0:T(8,128)(2,1)}) %reduce-scatter.4.cloned.1.call-update) | async-done | bytes 1982480 | tf_op jit(solution)/shard_map/reduce_scatter | solution.py:114
  514.1 58.5 %reduce-scatter.6.cloned.1.call-done = bf16[1,1408,768]{2,1,0:T(8,128)(2,1)} async-done(((bf16[1,1408,1536]{2,1,0:T(8,128)(2,1)}), bf16[1,1408,768]{2,1,0:T(8,128)(2,1)}) %reduce-scatter.6.cloned.1.call-update) | async-done | bytes 2162704 | tf_op jit(solution)/shard_map/reduce_scatter | solution.py:117
  572.7 58.7 %reduce-scatter.8.cloned.1.call-done = bf16[1,768,1408]{2,1,0:T(8,128)(2,1)} async-done(((bf16[1,1536,1408]{2,1,0:T(8,128)(2,1)}), bf16[1,768,1408]{2,1,0:T(8,128)(2,1)}) %reduce-scatter.8.cloned.1.call-update) | async-done | bytes 2162704 | tf_op jit(solution)/shard_map/reduce_scatter | solution.py:120
  (167 shorter events, 68.6 us)
Async XLA Ops:
  7.2 63.3 %all-gather.7.cloned.1.call-start = ((), (), s32[]{:S(2)}) async-start(), calls=%async_computation.4 | async-start | bytes 6488064 | tf_op jit(solution)/shard_map/all_gather | solution.py:43
  7.9 122.3 %all-gather.5.cloned.1.call-start = ((), (), s32[]{:S(2)}) async-start(), calls=%async_computation.3 | async-start | bytes 6488064 | tf_op jit(solution)/shard_map/all_gather | solution.py:44
  8.7 161.8 %all-reduce.5.cloned.1.call-start = ((), (), s32[]{:S(2)}) async-start(), calls=%async_computation.5 | async-start | bytes 1441792 | tf_op jit(solution)/shard_map/psum | solution.py:81
  9.7 64.8 %copy-start.17 = (bf16[128,1408]{1,0:T(8,128)(2,1)}, bf16[128,1408]{1,0:T(8,128)(2,1)S(1)}, u32[]{:S(2)}) copy-start(bf16[128,1408]{1,0:T(8,128)(2,1)S(1)} %gather_fusion.4) | copy-start | bytes 1081348
  70.5 64.5 %slice-start = ((s8[4325376]{0:T(1024)(128)(4,1)}), s8[131072]{0:T(1024)(128)(4,1)S(1)}, s32[]{:S(2)}) async-start(s8[4325376]{0:T(1024)(128)(4,1)} %bitcast.149), calls=%async_computation.14 | async-start | bytes 262144
  137.4 88.7 %all-gather.11.cloned.1.call-start = ((), (), s32[]{:S(2)}) async-start(), calls=%async_computation.7 | async-start | bytes 5947392 | tf_op jit(solution)/shard_map/all_gather | solution.py:42
  138.0 111.2 %all-gather.9.cloned.1.call-start = ((), (), s32[]{:S(2)}) async-start(), calls=%async_computation.6 | async-start | bytes 1622016 | tf_op jit(solution)/shard_map/all_gather | solution.py:51
  138.6 173.8 %all-reduce.7.cloned.1.call-start = ((), (), s32[]{:S(2)}) async-start(), calls=%async_computation.8 | async-start | bytes 1441792 | tf_op jit(solution)/shard_map/psum | solution.py:81
  229.5 1.5 collective-permute-start.1
  230.5 28.8 %copy-start.19 = (bf16[128,1408]{1,0:T(8,128)(2,1)}, bf16[128,1408]{1,0:T(8,128)(2,1)S(1)}, u32[]{:S(2)}) copy-start(bf16[128,1408]{1,0:T(8,128)(2,1)S(1)} %gather_fusion.5) | copy-start | bytes 1081348
  230.9 21.0 %collective-permute-start.2 = (bf16[128,704]{0,1:T(8,128)(2,1)S(1)}, bf16[128,704]{0,1:T(8,128)(2,1)S(1)}, u32[]{:S(2)}, u32[]{:S(2)}) collective-permute-start(bf16[128,704]{0,1:T(8,128)(2,1)S(1)} %collective-permute-done.1), channel_id=1, source_target_pairs={{0,8},{4,12},{8,0},{12,4},{16,24},{20,28},{24,16},{28,20},{1,9},{5... | collective-permute-start | bytes 540680 | tf_op jit(solution)/shard_map/ppermute | solution.py:13
  250.7 8.6 %collective-permute-start = (bf16[128,704]{0,1:T(8,128)(2,1)S(1)}, bf16[128,704]{0,1:T(8,128)(2,1)S(1)}, u32[]{:S(2)}, u32[]{:S(2)}) collective-permute-start(bf16[128,704]{0,1:T(8,128)(2,1)S(1)} %get-tuple-element.11), channel_id=1, source_target_pairs={{4,0},{8,4},{12,8},{16,12},{20,16},{24,20},{28,24},{5,1},{9,5},{13... | collective-permute-start | bytes 540680 | tf_op jit(solution)/shard_map/ppermute | solution.py:19
  252.0 14.2 %collective-permute-start.3 = (bf16[128,704]{0,1:T(8,128)(2,1)S(1)}, bf16[128,704]{0,1:T(8,128)(2,1)S(1)}, u32[]{:S(2)}, u32[]{:S(2)}) collective-permute-start(bf16[128,704]{0,1:T(8,128)(2,1)S(1)} %collective-permute-done.2), channel_id=1, source_target_pairs={{0,16},{4,20},{8,24},{12,28},{16,0},{20,4},{24,8},{28,12},{1,17},{... | collective-permute-start | bytes 540680 | tf_op jit(solution)/shard_map/ppermute | solution.py:13
  280.0 103.7 %all-reduce.9.cloned.1.call-start = ((), (), s32[]{:S(2)}) async-start(), calls=%async_computation.9 | async-start | bytes 1441792 | tf_op jit(solution)/shard_map/psum | solution.py:81
  317.1 1.5 collective-permute-start.5
  318.6 6.6 %collective-permute-start.6 = (bf16[128,704]{0,1:T(8,128)(2,1)S(1)}, bf16[128,704]{0,1:T(8,128)(2,1)S(1)}, u32[]{:S(2)}, u32[]{:S(2)}) collective-permute-start(bf16[128,704]{0,1:T(8,128)(2,1)S(1)} %collective-permute-done.5), channel_id=1, source_target_pairs={{0,8},{4,12},{8,0},{12,4},{16,24},{20,28},{24,16},{28,20},{1,9},{5... | collective-permute-start | bytes 540680 | tf_op jit(solution)/shard_map/ppermute | solution.py:13
  320.9 10.7 %copy-start.21 = (bf16[128,1408]{1,0:T(8,128)(2,1)}, bf16[128,1408]{1,0:T(8,128)(2,1)S(1)}, u32[]{:S(2)}) copy-start(bf16[128,1408]{1,0:T(8,128)(2,1)S(1)} %gather_fusion.6) | copy-start | bytes 1081348
  321.2 10.5 %collective-permute-start.4 = (bf16[128,704]{0,1:T(8,128)(2,1)S(1)}, bf16[128,704]{0,1:T(8,128)(2,1)S(1)}, u32[]{:S(2)}, u32[]{:S(2)}) collective-permute-start(bf16[128,704]{0,1:T(8,128)(2,1)S(1)} %get-tuple-element.9), channel_id=1, source_target_pairs={{4,0},{8,4},{12,8},{16,12},{20,16},{24,20},{28,24},{5,1},{9,5},{13... | collective-permute-start | bytes 540680 | tf_op jit(solution)/shard_map/ppermute | solution.py:19
  325.1 11.5 %collective-permute-start.7 = (bf16[128,704]{0,1:T(8,128)(2,1)S(1)}, bf16[128,704]{0,1:T(8,128)(2,1)S(1)}, u32[]{:S(2)}, u32[]{:S(2)}) collective-permute-start(bf16[128,704]{0,1:T(8,128)(2,1)S(1)} %collective-permute-done.6), channel_id=1, source_target_pairs={{0,16},{4,20},{8,24},{12,28},{16,0},{20,4},{24,8},{28,12},{1,17},{... | collective-permute-start | bytes 540680 | tf_op jit(solution)/shard_map/ppermute | solution.py:13
  343.3 5.1 slice-start.4
  343.4 40.4 %copy-start.3 = (bf16[128,1408]{1,0:T(8,128)(2,1)}, bf16[128,1408]{1,0:T(8,128)(2,1)S(1)}, u32[]{:S(2)}) copy-start(bf16[128,1408]{1,0:T(8,128)(2,1)S(1)} %bitcast_select_fusion.1) | copy-start | bytes 1081348
  350.8 104.2 %all-reduce.11.cloned.1.call-start = ((), (), s32[]{:S(2)}) async-start(), calls=%async_computation.10 | async-start | bytes 1441792 | tf_op jit(solution)/shard_map/psum | solution.py:81
  388.5 1.5 collective-permute-start.9
  389.9 6.6 %collective-permute-start.10 = (bf16[128,704]{0,1:T(8,128)(2,1)S(1)}, bf16[128,704]{0,1:T(8,128)(2,1)S(1)}, u32[]{:S(2)}, u32[]{:S(2)}) collective-permute-start(bf16[128,704]{0,1:T(8,128)(2,1)S(1)} %collective-permute-done.9), channel_id=1, source_target_pairs={{0,8},{4,12},{8,0},{12,4},{16,24},{20,28},{24,16},{28,20},{1,9},{5... | collective-permute-start | bytes 540680 | tf_op jit(solution)/shard_map/ppermute | solution.py:13
  392.3 10.7 %copy-start.22 = (bf16[128,1408]{1,0:T(8,128)(2,1)}, bf16[128,1408]{1,0:T(8,128)(2,1)S(1)}, u32[]{:S(2)}) copy-start(bf16[128,1408]{1,0:T(8,128)(2,1)S(1)} %gather_fusion.7) | copy-start | bytes 1081348
  392.6 10.5 %collective-permute-start.8 = (bf16[128,704]{0,1:T(8,128)(2,1)S(1)}, bf16[128,704]{0,1:T(8,128)(2,1)S(1)}, u32[]{:S(2)}, u32[]{:S(2)}) collective-permute-start(bf16[128,704]{0,1:T(8,128)(2,1)S(1)} %get-tuple-element.7), channel_id=1, source_target_pairs={{4,0},{8,4},{12,8},{16,12},{20,16},{24,20},{28,24},{5,1},{9,5},{13... | collective-permute-start | bytes 540680 | tf_op jit(solution)/shard_map/ppermute | solution.py:19
  396.5 11.5 %collective-permute-start.11 = (bf16[128,704]{0,1:T(8,128)(2,1)S(1)}, bf16[128,704]{0,1:T(8,128)(2,1)S(1)}, u32[]{:S(2)}, u32[]{:S(2)}) collective-permute-start(bf16[128,704]{0,1:T(8,128)(2,1)S(1)} %collective-permute-done.10), channel_id=1, source_target_pairs={{0,16},{4,20},{8,24},{12,28},{16,0},{20,4},{24,8},{28,12},{1,17},{... | collective-permute-start | bytes 540680 | tf_op jit(solution)/shard_map/ppermute | solution.py:13
  414.3 5.3 slice-start.6
  422.0 92.1 %reduce-scatter.4.cloned.1.call-start = ((), (), s32[]{:S(2)}) async-start(), calls=%async_computation.11 | async-start | bytes 5947392 | tf_op jit(solution)/shard_map/reduce_scatter | solution.py:114
  462.0 110.6 %reduce-scatter.6.cloned.1.call-start = ((), (), s32[]{:S(2)}) async-start(), calls=%async_computation.12 | async-start | bytes 6488064 | tf_op jit(solution)/shard_map/reduce_scatter | solution.py:117
  469.2 162.2 %reduce-scatter.8.cloned.1.call-start = ((), (), s32[]{:S(2)}) async-start(), calls=%async_computation.13 | async-start | bytes 6488064 | tf_op jit(solution)/shard_map/reduce_scatter | solution.py:120
  475.4 156.0 %copy-start.1 = (bf16[1,128,1408]{2,1,0:T(8,128)(2,1)S(1)}, bf16[1,128,1408]{2,1,0:T(8,128)(2,1)}, u32[]{:S(2)}) copy-start(bf16[1,128,1408]{2,1,0:T(8,128)(2,1)} %param.9) | copy-start | bytes 1081348
  (28 other events, 62.0 us)
Sparse Core Ops, SparseCore 0:
  9.5 60.9 all-gather.6
  72.0 58.1 all-gather.4
  137.6 32.9 all-reduce.4
  171.9 54.1 all-gather.10
  227.5 21.6 all-gather.8
  280.2 32.1 all-reduce.6
  350.9 32.8 all-reduce.8
  422.1 32.8 all-reduce.10
  462.2 51.8 reduce-scatter.3
  516.8 55.7 reduce-scatter.5
  575.6 55.7 reduce-scatter.7
where the time goes:
time: 639 us; the launch traced here: 638 us
  waiting for transfers between devices  479 us (75%)
  matrix products  72.9 us (11%)
  blocking collectives  26.9 us (4%)
  local copies, waits for them, and re-layouts  21 us (3%)
  starting transfers between devices  17.4 us (3%)
  between operations  14.5 us (2%)
    psum x4, waiting for transfers between devices, body(): back_mixed = upstream.astype(jnp.float32) + lax.psum(partial_back, 'tensor')  120 us
    reduce_scatter x1, waiting for transfers between devices, body(): lax.psum_scatter(down_total[None].astype(jnp.bfloat16), 'replica', scatte...  58.7 us
    reduce_scatter x1, waiting for transfers between devices, body(): lax.psum_scatter(up_total[None].astype(jnp.bfloat16), 'replica', scatter_...  58.5 us
    all_gather x1, waiting for transfers between devices, body(): lax.all_gather(w_down, 'replica', axis=1, tiled=True)  55.8 us
    all_gather x1, waiting for transfers between devices, body(): lax.all_gather(w_proj, 'replica', axis=2, tiled=True)  54.4 us
    all_gather x1, waiting for transfers between devices, body(): lax.all_gather(w_up, 'replica', axis=2, tiled=True)  52.6 us
    reduce_scatter x1, waiting for transfers between devices, body(): lax.psum_scatter(proj_total[None].astype(jnp.bfloat16), 'replica', scatte...  34.5 us
    ppermute x9, waiting for transfers between devices, from_partner(): return lax.ppermute(value, axis, pairs)  25.6 us
  transfers between devices with their start and end apart: 23, of which 19 were waited for; matrix products, arithmetic and copies ran while one was open for 8% of the time, Pallas kernels for 0%

commit v1 on v0

--- a/solution.py
+++ b/solution.py
@@ -78,7 +78,8 @@
         partial_back = jnp.einsum(
             "mf,df->md", back_hidden, up_local, preferred_element_type=jnp.float32
         )
-        back_mixed = upstream.astype(jnp.float32) + lax.psum(partial_back, "tensor")
+        raise_heaps = lambda vector, a_name: lax.all_gather(vector, a_name).sum(axis=0)
+        back_mixed = upstream.astype(jnp.float32) + raise_heaps(partial_back, "tensor")
         mixed_grad = back_mixed.astype(jnp.bfloat16)
         input_grad = jnp.einsum(
             "mj,kij->mki", mixed_grad, proj_local, preferred_element_type=jnp.float32

time: 639 us -> 588 us (0.920)
  waiting for transfers between devices: 479 us -> 429 us
  other arithmetic: 6.25 us -> 12.8 us
    psum x4 -> x0, waiting for transfers between devices: 120 us -> none  [body(): back_mixed = upstream.astype(jnp.float32) + lax.psum(partial_back, 'tensor')]
    all_gather x0 -> x4, waiting for transfers between devices: none -> 76.8 us  [body(): lax.all_gather(vector, a_name).sum(axis=0)]
    reduce_scatter x1, waiting for transfers between devices: 34.5 us -> 54.8 us  [body(): lax.psum_scatter(proj_total[None].astype(jnp.bfloat16), 'replica', scatte...]
    all_gather x1, waiting for transfers between devices: 16.7 us -> 0.01 us  [body(): lax.all_gather(loss_grads, 'tensor', axis=2, tiled=True)]
    reduce_scatter x1, waiting for transfers between devices: 58.5 us -> 46.5 us  [body(): lax.psum_scatter(up_total[None].astype(jnp.bfloat16), 'replica', scatter_...]
  transfers between devices with their start and end apart: 23 -> 23, of which waited for: 19 -> 19; matrix products, arithmetic and copies ran while one was open for 8% -> 10% of each run, Pallas kernels for 0% -> 0%
where the time goes in v1:
time: 588 us
  waiting for transfers between devices  429 us (73%)
  matrix products  69.4 us (12%)
  blocking collectives  27 us (5%)
  local copies, waits for them, and re-layouts  17.8 us (3%)
  starting transfers between devices  17.1 us (3%)
  between operations  14.6 us (2%)
  other arithmetic  12.8 us (2%)
    all_gather x4, waiting for transfers between devices, body(): lax.all_gather(vector, a_name).sum(axis=0)  76.8 us
    reduce_scatter x1, waiting for transfers between devices, body(): lax.psum_scatter(down_total[None].astype(jnp.bfloat16), 'replica', scatte...  58.6 us
    all_gather x1, waiting for transfers between devices, body(): lax.all_gather(w_down, 'replica', axis=1, tiled=True)  55.8 us
    reduce_scatter x1, waiting for transfers between devices, body(): lax.psum_scatter(proj_total[None].astype(jnp.bfloat16), 'replica', scatte...  54.8 us
    all_gather x1, waiting for transfers between devices, body(): lax.all_gather(w_proj, 'replica', axis=2, tiled=True)  53.8 us
    all_gather x1, waiting for transfers between devices, body(): lax.all_gather(w_up, 'replica', axis=2, tiled=True)  52.6 us
    reduce_scatter x1, waiting for transfers between devices, body(): lax.psum_scatter(up_total[None].astype(jnp.bfloat16), 'replica', scatter_...  46.5 us
    ppermute x9, waiting for transfers between devices, from_partner(): return lax.ppermute(value, axis, pairs)  27.3 us
  transfers between devices with their start and end apart: 23, of which 19 were waited for; matrix products, arithmetic and copies ran while one was open for 10% of the time, Pallas kernels for 0%

profile of v1, /device:TPU:0, one launch (start us, length us, event | category | flops | bytes accessed | tf_op | source)
XLA Modules:
  0.0 587.5 jit_solution(4379998357766115841)
XLA Ops:
  9.7 8.2 %all_gather.48 = bf16[1,128,1408]{1,2,0:T(8,128)(2,1)S(1)} all-gather(bf16[1,128,704]{1,2,0:T(8,128)(2,1)S(1)} %copy-done.22), channel_id=1, replica_groups=mesh['section'=8,'tensor'=2,'replica'=2] {'tensor'}, dimensions={2}, use_global_device_ids=true | all-gather | bytes 540672 | tf_op jit(solution)/shard_map/all_gather | solution.py:50
  17.9 52.6 %all-gather.15.cloned.1.call-done = bf16[1,1408,1536]{2,1,0:T(8,128)(2,1)} async-done(((bf16[1,1408,768]{2,1,0:T(8,128)(2,1)}), bf16[1,1408,1536]{2,1,0:T(8,128)(2,1)}) %all-gather.15.cloned.1.call-update) | async-done | bytes 4325392 | tf_op jit(solution)/shard_map/all_gather | solution.py:43
  70.5 4.0 multiply_convert_fusion.3
  74.5 55.8 %all-gather.13.cloned.1.call-done = bf16[1,1536,1408]{2,1,0:T(8,128)(2,1)} async-done(((bf16[1,768,1408]{2,1,0:T(8,128)(2,1)}), bf16[1,1536,1408]{2,1,0:T(8,128)(2,1)}) %all-gather.13.cloned.1.call-update) | async-done | bytes 4325392 | tf_op jit(solution)/shard_map/all_gather | solution.py:44
  130.3 4.0 fusion.56
  137.9 24.6 %all-gather.21.cloned.1.call-done = f32[256,1408]{1,0:T(8,128)} async-done(((f32[128,1408]{1,0:T(8,128)}), f32[256,1408]{1,0:T(8,128)}) %all-gather.21.cloned.1.call-update) | async-done | bytes 1441808 | tf_op jit(solution)/shard_map/all_gather | solution.py:81
  164.4 53.8 %all-gather.19.cloned.1.call-done = bf16[1,2,704,1408]{3,2,1,0:T(8,128)(2,1)} async-done(((bf16[1,2,352,1408]{3,2,1,0:T(8,128)(2,1)}), bf16[1,2,704,1408]{3,2,1,0:T(8,128)(2,1)}) %all-gather.19.cloned.1.call-update) | async-done | bytes 3964944 | tf_op jit(solution)/shard_map/all_gather | solution.py:42
  218.1 3.3 fusion.100
  226.7 2.9 collective-permute-done.2
  232.0 4.1 multiply_convert_fusion.2
  236.1 4.8 collective-permute-done.3
  241.0 6.4 %all_gather.55 = bf16[128,1408]{0,1:T(8,128)(2,1)S(1)} all-gather(bf16[128,704]{0,1:T(8,128)(2,1)S(1)} %add_convert_fusion.6), channel_id=1, replica_groups=mesh['section'=8,'tensor'=2,'replica'=2] {'tensor'}, dimensions={1}, use_global_device_ids=true | all-gather | bytes 540672 | tf_op jit(solution)/shard_map/all_gather | solution.py:99
  248.6 4.3 fusion.53
  256.0 25.7 %all-gather.23.cloned.1.call-done = f32[256,1408]{1,0:T(8,128)} async-done(((f32[128,1408]{1,0:T(8,128)}), f32[256,1408]{1,0:T(8,128)}) %all-gather.23.cloned.1.call-update) | async-done | bytes 1441808 | tf_op jit(solution)/shard_map/all_gather | solution.py:81
  283.6 3.5 fusion.103
  292.8 2.4 collective-permute-done.6
  297.6 4.0 multiply_convert_fusion.1
  301.6 5.2 collective-permute-done.7
  306.9 6.2 %all_gather.58 = bf16[128,1408]{0,1:T(8,128)(2,1)S(1)} all-gather(bf16[128,704]{0,1:T(8,128)(2,1)S(1)} %add_convert_fusion.5), channel_id=1, replica_groups=mesh['section'=8,'tensor'=2,'replica'=2] {'tensor'}, dimensions={1}, use_global_device_ids=true | all-gather | bytes 540672 | tf_op jit(solution)/shard_map/all_gather | solution.py:99
  319.1 25.7 %all-gather.25.cloned.1.call-done = f32[256,1408]{1,0:T(8,128)} async-done(((f32[128,1408]{1,0:T(8,128)}), f32[256,1408]{1,0:T(8,128)}) %all-gather.25.cloned.1.call-update) | async-done | bytes 1441808 | tf_op jit(solution)/shard_map/all_gather | solution.py:81
  347.7 3.5 fusion.106
  356.6 2.6 collective-permute-done.10
  361.7 4.0 multiply_convert_fusion
  365.6 5.2 collective-permute-done.11
  370.9 6.3 %all_gather.61 = bf16[128,1408]{0,1:T(8,128)(2,1)S(1)} all-gather(bf16[128,704]{0,1:T(8,128)(2,1)S(1)} %add_convert_fusion.4), channel_id=1, replica_groups=mesh['section'=8,'tensor'=2,'replica'=2] {'tensor'}, dimensions={1}, use_global_device_ids=true | all-gather | bytes 540672 | tf_op jit(solution)/shard_map/all_gather | solution.py:99
  383.2 6.0 %fusion = bf16[1,1408,1536]{2,1,0:T(8,128)(2,1)} fusion(bf16[128,1536]{1,0:T(8,128)(2,1)} %copy-done.15, bf16[128,1536]{1,0:T(8,128)(2,1)} %copy-done.14, bf16[128,1536]{1,0:T(8,128)(2,1)S(1)} %copy-done.13, bf16[128,1536]{1,0:T(8,128)(2,1)S(1)} %copy-done.11, bf16[128,1408]{1,0:T(8,128)(2,1)} %copy-done.21, bf16[128,1408]{1,0:T(8,128)(2,1)} %copy-done.20, ...), kind=kOutput, calls=%fused_computation.10 | convolution fusion | flops 2228813824 | bytes 7340032 | tf_op jit(solution)/shard_map/md,mf->df/dot_general | solution.py:110
  390.5 5.9 fusion.1
  410.7 5.5 fusion.34
  416.3 4.8 fusion.112
  421.1 46.5 %reduce-scatter.6.cloned.1.call-done = bf16[1,1408,768]{2,1,0:T(8,128)(2,1)} async-done(((bf16[1,1408,1536]{2,1,0:T(8,128)(2,1)}), bf16[1,1408,768]{2,1,0:T(8,128)(2,1)}) %reduce-scatter.6.cloned.1.call-update) | async-done | bytes 2162704 | tf_op jit(solution)/shard_map/reduce_scatter | solution.py:118
  467.6 58.6 %reduce-scatter.8.cloned.1.call-done = bf16[1,768,1408]{2,1,0:T(8,128)(2,1)} async-done(((bf16[1,1536,1408]{2,1,0:T(8,128)(2,1)}), bf16[1,768,1408]{2,1,0:T(8,128)(2,1)}) %reduce-scatter.8.cloned.1.call-update) | async-done | bytes 2162704 | tf_op jit(solution)/shard_map/reduce_scatter | solution.py:121
  526.2 54.8 %reduce-scatter.4.cloned.1.call-done = bf16[1,2,352,1408]{3,2,1,0:T(8,128)(2,1)} async-done(((bf16[1,2,704,1408]{3,2,1,0:T(8,128)(2,1)}), bf16[1,2,352,1408]{3,2,1,0:T(8,128)(2,1)}) %reduce-scatter.4.cloned.1.call-update) | async-done | bytes 1982480 | tf_op jit(solution)/shard_map/reduce_scatter | solution.py:115
  (171 shorter events, 68.0 us)
Async XLA Ops:
  7.2 63.3 %all-gather.15.cloned.1.call-start = ((), (), s32[]{:S(2)}) async-start(), calls=%async_computation.4 | async-start | bytes 6488064 | tf_op jit(solution)/shard_map/all_gather | solution.py:43
  7.9 122.3 %all-gather.13.cloned.1.call-start = ((), (), s32[]{:S(2)}) async-start(), calls=%async_computation.3 | async-start | bytes 6488064 | tf_op jit(solution)/shard_map/all_gather | solution.py:44
  8.7 153.9 %all-gather.21.cloned.1.call-start = ((), (), s32[]{:S(2)}) async-start(), calls=%async_computation.10 | async-start | bytes 2162688 | tf_op jit(solution)/shard_map/all_gather | solution.py:81
  9.7 64.8 %copy-start.17 = (bf16[128,1408]{1,0:T(8,128)(2,1)}, bf16[128,1408]{1,0:T(8,128)(2,1)S(1)}, u32[]{:S(2)}) copy-start(bf16[128,1408]{1,0:T(8,128)(2,1)S(1)} %gather_fusion.4) | copy-start | bytes 1081348
  70.5 63.8 %slice-start = ((s8[4325376]{0:T(1024)(128)(4,1)}), s8[131072]{0:T(1024)(128)(4,1)S(1)}, s32[]{:S(2)}) async-start(s8[4325376]{0:T(1024)(128)(4,1)} %bitcast.167), calls=%async_computation.14 | async-start | bytes 262144
  136.7 81.4 %all-gather.19.cloned.1.call-start = ((), (), s32[]{:S(2)}) async-start(), calls=%async_computation.6 | async-start | bytes 5947392 | tf_op jit(solution)/shard_map/all_gather | solution.py:42
  137.3 110.1 %all-gather.17.cloned.1.call-start = ((), (), s32[]{:S(2)}) async-start(), calls=%async_computation.5 | async-start | bytes 1622016 | tf_op jit(solution)/shard_map/all_gather | solution.py:51
  137.9 143.8 %all-gather.23.cloned.1.call-start = ((), (), s32[]{:S(2)}) async-start(), calls=%async_computation.11 | async-start | bytes 2162688 | tf_op jit(solution)/shard_map/all_gather | solution.py:81
  221.5 1.5 collective-permute-start.1
  223.0 6.6 %collective-permute-start.2 = (bf16[128,704]{0,1:T(8,128)(2,1)S(1)}, bf16[128,704]{0,1:T(8,128)(2,1)S(1)}, u32[]{:S(2)}, u32[]{:S(2)}) collective-permute-start(bf16[128,704]{0,1:T(8,128)(2,1)S(1)} %collective-permute-done.1), channel_id=1, source_target_pairs={{0,8},{4,12},{8,0},{12,4},{16,24},{20,28},{24,16},{28,20},{1,9},{5... | collective-permute-start | bytes 540680 | tf_op jit(solution)/shard_map/ppermute | solution.py:13
  225.4 10.8 %copy-start.19 = (bf16[128,1408]{1,0:T(8,128)(2,1)}, bf16[128,1408]{1,0:T(8,128)(2,1)S(1)}, u32[]{:S(2)}) copy-start(bf16[128,1408]{1,0:T(8,128)(2,1)S(1)} %gather_fusion.5) | copy-start | bytes 1081348
  225.4 10.7 %collective-permute-start = (bf16[128,704]{0,1:T(8,128)(2,1)S(1)}, bf16[128,704]{0,1:T(8,128)(2,1)S(1)}, u32[]{:S(2)}, u32[]{:S(2)}) collective-permute-start(bf16[128,704]{0,1:T(8,128)(2,1)S(1)} %get-tuple-element.8), channel_id=1, source_target_pairs={{4,0},{8,4},{12,8},{16,12},{20,16},{24,20},{28,24},{5,1},{9,5},{13... | collective-permute-start | bytes 540680 | tf_op jit(solution)/shard_map/ppermute | solution.py:19
  229.6 11.3 %collective-permute-start.3 = (bf16[128,704]{0,1:T(8,128)(2,1)S(1)}, bf16[128,704]{0,1:T(8,128)(2,1)S(1)}, u32[]{:S(2)}, u32[]{:S(2)}) collective-permute-start(bf16[128,704]{0,1:T(8,128)(2,1)S(1)} %collective-permute-done.2), channel_id=1, source_target_pairs={{0,16},{4,20},{8,24},{12,28},{16,0},{20,4},{24,8},{28,12},{1,17},{... | collective-permute-start | bytes 540680 | tf_op jit(solution)/shard_map/ppermute | solution.py:13
  256.0 88.8 %all-gather.25.cloned.1.call-start = ((), (), s32[]{:S(2)}) async-start(), calls=%async_computation.12 | async-start | bytes 2162688 | tf_op jit(solution)/shard_map/all_gather | solution.py:81
  287.1 1.5 collective-permute-start.5
  288.6 6.6 %collective-permute-start.6 = (bf16[128,704]{0,1:T(8,128)(2,1)S(1)}, bf16[128,704]{0,1:T(8,128)(2,1)S(1)}, u32[]{:S(2)}, u32[]{:S(2)}) collective-permute-start(bf16[128,704]{0,1:T(8,128)(2,1)S(1)} %collective-permute-done.5), channel_id=1, source_target_pairs={{0,8},{4,12},{8,0},{12,4},{16,24},{20,28},{24,16},{28,20},{1,9},{5... | collective-permute-start | bytes 540680 | tf_op jit(solution)/shard_map/ppermute | solution.py:13
  291.0 23.2 %slice-start.8 = ((s8[4325376]{0:T(1024)(128)(4,1)}), s8[4194304]{0:T(1024)(128)(4,1)S(1)}, s32[]{:S(2)}) async-start(s8[4325376]{0:T(1024)(128)(4,1)} %bitcast.184), calls=%async_computation.22 | async-start | bytes 8388608
  291.0 23.2 %slice-start.9 = ((s8[4325376]{0:T(1024)(128)(4,1)}), s8[131072]{0:T(1024)(128)(4,1)S(1)}, s32[]{:S(2)}) async-start(s8[4325376]{0:T(1024)(128)(4,1)} %bitcast.184), calls=%async_computation.23 | async-start | bytes 262144
  291.0 10.5 %collective-permute-start.4 = (bf16[128,704]{0,1:T(8,128)(2,1)S(1)}, bf16[128,704]{0,1:T(8,128)(2,1)S(1)}, u32[]{:S(2)}, u32[]{:S(2)}) collective-permute-start(bf16[128,704]{0,1:T(8,128)(2,1)S(1)} %get-tuple-element.6), channel_id=1, source_target_pairs={{4,0},{8,4},{12,8},{16,12},{20,16},{24,20},{28,24},{5,1},{9,5},{13... | collective-permute-start | bytes 540680 | tf_op jit(solution)/shard_map/ppermute | solution.py:19
  295.2 11.6 %collective-permute-start.7 = (bf16[128,704]{0,1:T(8,128)(2,1)S(1)}, bf16[128,704]{0,1:T(8,128)(2,1)S(1)}, u32[]{:S(2)}, u32[]{:S(2)}) collective-permute-start(bf16[128,704]{0,1:T(8,128)(2,1)S(1)} %collective-permute-done.6), channel_id=1, source_target_pairs={{0,16},{4,20},{8,24},{12,28},{16,0},{20,4},{24,8},{28,12},{1,17},{... | collective-permute-start | bytes 540680 | tf_op jit(solution)/shard_map/ppermute | solution.py:13
  319.1 89.8 %all-gather.27.cloned.1.call-start = ((), (), s32[]{:S(2)}) async-start(), calls=%async_computation.13 | async-start | bytes 2162688 | tf_op jit(solution)/shard_map/all_gather | solution.py:81
  351.2 1.5 collective-permute-start.9
  352.6 6.6 %collective-permute-start.10 = (bf16[128,704]{0,1:T(8,128)(2,1)S(1)}, bf16[128,704]{0,1:T(8,128)(2,1)S(1)}, u32[]{:S(2)}, u32[]{:S(2)}) collective-permute-start(bf16[128,704]{0,1:T(8,128)(2,1)S(1)} %collective-permute-done.9), channel_id=1, source_target_pairs={{0,8},{4,12},{8,0},{12,4},{16,24},{20,28},{24,16},{28,20},{1,9},{5... | collective-permute-start | bytes 540680 | tf_op jit(solution)/shard_map/ppermute | solution.py:13
  355.1 23.2 %slice-start.10 = ((s8[4325376]{0:T(1024)(128)(4,1)}), s8[4194304]{0:T(1024)(128)(4,1)S(1)}, s32[]{:S(2)}) async-start(s8[4325376]{0:T(1024)(128)(4,1)} %bitcast.186), calls=%async_computation.24 | async-start | bytes 8388608
  355.1 23.2 %slice-start.11 = ((s8[4325376]{0:T(1024)(128)(4,1)}), s8[131072]{0:T(1024)(128)(4,1)S(1)}, s32[]{:S(2)}) async-start(s8[4325376]{0:T(1024)(128)(4,1)} %bitcast.186), calls=%async_computation.25 | async-start | bytes 262144
  355.1 10.5 %collective-permute-start.8 = (bf16[128,704]{0,1:T(8,128)(2,1)S(1)}, bf16[128,704]{0,1:T(8,128)(2,1)S(1)}, u32[]{:S(2)}, u32[]{:S(2)}) collective-permute-start(bf16[128,704]{0,1:T(8,128)(2,1)S(1)} %get-tuple-element.4), channel_id=1, source_target_pairs={{4,0},{8,4},{12,8},{16,12},{20,16},{24,20},{28,24},{5,1},{9,5},{13... | collective-permute-start | bytes 540680 | tf_op jit(solution)/shard_map/ppermute | solution.py:19
  359.2 11.6 %collective-permute-start.11 = (bf16[128,704]{0,1:T(8,128)(2,1)S(1)}, bf16[128,704]{0,1:T(8,128)(2,1)S(1)}, u32[]{:S(2)}, u32[]{:S(2)}) collective-permute-start(bf16[128,704]{0,1:T(8,128)(2,1)S(1)} %collective-permute-done.10), channel_id=1, source_target_pairs={{0,16},{4,20},{8,24},{12,28},{16,0},{20,4},{24,8},{28,12},{1,17},{... | collective-permute-start | bytes 540680 | tf_op jit(solution)/shard_map/ppermute | solution.py:13
  378.2 11.2 %copy-start.8 = (bf16[128,1408]{0,1:T(8,128)(2,1)}, bf16[128,1408]{0,1:T(8,128)(2,1)S(1)}, u32[]{:S(2)}) copy-start(bf16[128,1408]{0,1:T(8,128)(2,1)S(1)} %fusion.138) | copy-start | bytes 1081348
  383.1 84.4 %reduce-scatter.6.cloned.1.call-start = ((), (), s32[]{:S(2)}) async-start(), calls=%async_computation.8 | async-start | bytes 6488064 | tf_op jit(solution)/shard_map/reduce_scatter | solution.py:118
  389.2 137.0 %reduce-scatter.8.cloned.1.call-start = ((), (), s32[]{:S(2)}) async-start(), calls=%async_computation.9 | async-start | bytes 6488064 | tf_op jit(solution)/shard_map/reduce_scatter | solution.py:121
  396.4 184.6 %reduce-scatter.4.cloned.1.call-start = ((), (), s32[]{:S(2)}) async-start(), calls=%async_computation.7 | async-start | bytes 5947392 | tf_op jit(solution)/shard_map/reduce_scatter | solution.py:115
  416.3 164.7 %copy-start.1 = (bf16[1,128,1408]{2,1,0:T(8,128)(2,1)S(1)}, bf16[1,128,1408]{2,1,0:T(8,128)(2,1)}, u32[]{:S(2)}) copy-start(bf16[1,128,1408]{2,1,0:T(8,128)(2,1)} %param.9) | copy-start | bytes 1081348
  (29 other events, 93.6 us)
Sparse Core Ops, SparseCore 0:
  9.5 60.9 all-gather.14
  72.0 58.1 all-gather.12
  136.8 25.6 all-gather.20
  164.0 54.1 all-gather.18
  219.5 21.6 all-gather.16
  256.1 25.5 all-gather.22
  319.2 25.5 all-gather.24
  383.3 25.5 all-gather.26
  411.7 55.7 reduce-scatter.5
  470.3 55.7 reduce-scatter.7
  529.0 51.8 reduce-scatter.3
